TPU v7x, 256 devices: a whole 4x4x8 slice. The times are simulated.
256 devices in a mesh: pool: 16 (over z, core), tensor: 16 (over y, x).
Axes of the slice: x: 4, y: 4, z: 8, core: 2. Of those that a mesh axis runs over, the one named last changes fastest.
Arguments:
- hidden: bfloat16 [8192, 14336], P('pool', 'tensor'), may hold values from -6 to 6
- down_weight: bfloat16 [14336, 8192], P('tensor', 'pool'), may hold values from -0.046875 to 0.046875
- adapter_shrink: bfloat16 [32, 14336, 64], P('pool', 'tensor'), may hold values from -0.046875 to 0.046875
- adapter_expand: bfloat16 [32, 8192, 64], P('pool', 'tensor'), may hold values from -0.75 to 0.75
- block_adapter: int32 [64], P('pool'), may hold values from 0 to 31, as said below
- block_rows: int32 [64], P('pool'), may hold values from 1 to 128, 6144 in all
Outputs:
- projected: bfloat16 [8192, 8192], P(('pool', 'tensor'))
Inputs may be any that keep to these rules, and one draw needn't show every extreme that they name: `block_adapter`: within each aligned run of 4 blocks (the rows of one pool index) no two blocks name adapters with the same a // 2. `block_rows`: some block is full.
All inputs are finite; a program needn't handle non-finite values.
Results may differ from a plain program's by a relative error of at most 0.02.
Values may be sent and summed in bfloat16 or wider, within the bound.
A program may use at most 128 MiB of HBM per device.

v0:
```python
import jax
import jax.numpy as jnp
from jax import lax
from jax.sharding import PartitionSpec as P

BLOCK = 128
adapter_scale_factor = 0.5


def shards(hidden, down_weight, adapter_shrink, adapter_expand, block_adapter, block_rows):
    input_rows, feat = hidden.shape
    block_count = block_adapter.shape[0]
    column_span = adapter_expand.shape[1]
    tensor_pos = lax.axis_index("tensor")
    tensor_count = lax.axis_size("tensor")
    own_rows = input_rows // tensor_count
    blocks = hidden.reshape(block_count, BLOCK, feat)
    partial_value = jnp.dot(
        hidden,
        lax.all_gather(down_weight, "pool", axis=1, tiled=True),
        preferred_element_type=jnp.float32,
    )
    total = lax.psum_scatter(
        partial_value.astype(jnp.bfloat16), "tensor", scatter_dimension=0, tiled=True
    ).astype(jnp.float32)
    shrink_piece = lax.all_gather(adapter_shrink, "pool", axis=0, tiled=True)
    expand_piece = lax.all_gather(adapter_expand, "pool", axis=0, tiled=True)
    idents = jnp.arange(shrink_piece.shape[0], dtype=jnp.int32)
    pick = (block_adapter[:, None] == idents[None, :]).astype(jnp.bfloat16)
    first = jnp.einsum("bk,kfr->bfr", pick, shrink_piece, preferred_element_type=jnp.float32)
    second = jnp.einsum("bk,kcr->bcr", pick, expand_piece, preferred_element_type=jnp.float32)
    shrink = jnp.einsum(
        "bnf,bfr->bnr", blocks, first.astype(jnp.bfloat16), preferred_element_type=jnp.float32
    )
    summed_shrink = lax.psum(shrink.astype(jnp.bfloat16), "tensor")
    enlarged_rows = jnp.einsum(
        "bnr,bcr->bnc",
        summed_shrink,
        second.astype(jnp.bfloat16),
        preferred_element_type=jnp.float32,
    )
    adapter_delta_columns = (
        (adapter_scale_factor * enlarged_rows).astype(jnp.bfloat16).reshape(input_rows, column_span)
    )
    delta_mine = lax.all_to_all(
        adapter_delta_columns, "tensor", split_axis=0, concat_axis=1, tiled=True
    )
    total = total + delta_mine.astype(jnp.float32)
    row_ids = tensor_pos * own_rows + jnp.arange(own_rows, dtype=jnp.int32)
    owning = (row_ids // BLOCK)[:, None] == jnp.arange(block_count, dtype=jnp.int32)[None, :]
    lengths = jnp.sum(jnp.where(owning, block_rows[None, :], 0), axis=1)
    valid = (row_ids % BLOCK < lengths).astype(jnp.float32)
    return (total * valid[:, None]).astype(jnp.bfloat16)


def solution(mesh):
    in_specs = (
        P("pool", "tensor"),
        P("tensor", "pool"),
        P("pool", "tensor", None),
        P("pool", "tensor", None),
        P("pool"),
        P("pool"),
    )
    out_specs = P(("pool", "tensor"), None)
    return jax.shard_map(shards, mesh=mesh, in_specs=in_specs, out_specs=out_specs, check_vma=False)
```

profile of v0, /device:TPU:2, one launch (start us, length us, event | category | flops | bytes accessed | tf_op | source)
XLA Modules:
  0.0 374.3 jit_solution(14904361085306204502)
XLA Ops:
  6.5 0.0 copy-start
  6.5 0.0 all-gather.6.cloned.1.call-start
  6.5 0.7 all-gather.6.cloned.1.call-update
  7.3 0.0 all-gather.4.cloned.1.call-start
  7.3 0.7 all-gather.4.cloned.1.call-update
  8.0 0.0 all-gather.8.cloned.1.call-start
  8.1 0.7 all-gather.8.cloned.1.call-update
  8.7 0.0 all-reduce.2.cloned.1.call-start
  8.8 45.0 %all-gather.6.cloned.1.call-done = bf16[32,896,64]{1,2,0:T(8,128)(2,1)} async-done(((bf16[2,896,64]{1,2,0:T(8,128)(2,1)}), bf16[32,896,64]{1,2,0:T(8,128)(2,1)}) %all-gather.6.cloned.1.call-update) | async-done | bytes 3670032 | tf_op jit(solution)/shard_map/all_gather | solution.py:26
  53.8 5.0 %fusion.5 = bf16[4,896,64]{1,0,2:T(4,128)(2,1)S(1)} fusion(bf16[32,896,64]{1,2,0:T(8,128)(2,1)} %all-gather.6.cloned.1.call-done, s32[4]{0:T(128)} %param.10), kind=kOutput, calls=%fused_computation.7 | convolution fusion | flops 14909568 | bytes 4128784 | tf_op jit(solution)/shard_map/bk,kfr->bfr/dot_general | solution.py:30
  58.8 0.0 copy-done
  58.8 1.1 fusion.11
  59.9 0.0 all-reduce.2.cloned.1.call-update
  59.9 0.0 reduce-scatter.2.cloned.1.call-start
  59.9 79.8 %all-gather.4.cloned.1.call-done = bf16[896,8192]{1,0:T(8,128)(2,1)} async-done(((bf16[896,512]{1,0:T(8,128)(2,1)}), bf16[896,8192]{1,0:T(8,128)(2,1)}) %all-gather.4.cloned.1.call-update) | async-done | bytes 14680080 | tf_op jit(solution)/shard_map/all_gather | solution.py:20
  139.8 16.5 %convolution_convert_fusion = bf16[512,8192]{1,0:T(8,128)(2,1)} fusion(bf16[512,896]{1,0:T(8,128)(2,1)S(1)} %copy-done, bf16[896,8192]{1,0:T(8,128)(2,1)} %all-gather.4.cloned.1.call-done), kind=kOutput, calls=%fused_computation | convolution fusion | flops 7520387072 | bytes 23986176 | tf_op jit(solution)/shard_map/dot_general | solution.py:18
  156.3 0.0 copy-start.1
  156.3 0.0 reduce-scatter.2.cloned.1.call-update
  156.3 0.0 copy-start.2
  156.3 23.6 %all-gather.8.cloned.1.call-done = bf16[32,512,64]{1,2,0:T(8,128)(2,1)} async-done(((bf16[2,512,64]{1,2,0:T(8,128)(2,1)}), bf16[32,512,64]{1,2,0:T(8,128)(2,1)}) %all-gather.8.cloned.1.call-update) | async-done | bytes 2097168 | tf_op jit(solution)/shard_map/all_gather | solution.py:27
  179.9 0.0 copy-done.1
  179.9 2.9 fusion.8
  182.8 89.2 %all-reduce.2.cloned.1.call-done = bf16[4,128,64]{1,2,0:T(8,128)(2,1)} async-done(((bf16[4,128,64]{1,2,0:T(8,128)(2,1)}), bf16[4,128,64]{1,2,0:T(8,128)(2,1)}) %all-reduce.2.cloned.1.call-update) | async-done | bytes 65552 | tf_op jit(solution)/shard_map/psum | solution.py:35
  272.0 2.0 fusion.4
  274.0 5.7 %all-to-all-start = ((bf16[16,32,512]{2,1,0:T(8,128)(2,1)}), bf16[16,32,512]{2,1,0:T(8,128)(2,1)S(1)}, u32[]{:S(2)}, u32[]{:S(2)}) async-start(bf16[16,32,512]{2,1,0:T(8,128)(2,1)} %bitcast.3), calls=%async_computation.1 | async-start | bytes 1048576 | tf_op jit(solution)/shard_map/all_to_all | solution.py:45
  279.7 0.0 copy-done.2
  279.8 0.1 select_reduce_fusion
  279.9 8.6 %all-to-all-done = bf16[16,32,512]{2,1,0:T(8,128)(2,1)S(1)} async-done(((bf16[16,32,512]{2,1,0:T(8,128)(2,1)}), bf16[16,32,512]{2,1,0:T(8,128)(2,1)S(1)}, u32[]{:S(2)}, u32[]{:S(2)}) %all-to-all-start) | async-done | bytes 524320 | tf_op jit(solution)/shard_map/all_to_all | solution.py:45
  288.5 0.1 convert_bitcast_fusion
  288.6 0.1 copy.14
  288.7 77.0 %reduce-scatter.2.cloned.1.call-done = bf16[32,8192]{1,0:T(8,128)(2,1)} async-done(((bf16[512,8192]{1,0:T(8,128)(2,1)}), bf16[32,8192]{1,0:T(8,128)(2,1)}) %reduce-scatter.2.cloned.1.call-update) | async-done | bytes 524304 | tf_op jit(solution)/shard_map/reduce_scatter | solution.py:23
  365.7 2.0 multiply_convert_fusion
  (2 shorter events, 0.0 us)
Async XLA Ops:
  6.5 52.2 %copy-start = (bf16[512,896]{1,0:T(8,128)(2,1)S(1)}, bf16[512,896]{1,0:T(8,128)(2,1)}, u32[]{:S(2)}) copy-start(bf16[512,896]{1,0:T(8,128)(2,1)} %param.6) | copy-start | bytes 2752516
  6.5 47.2 %all-gather.6.cloned.1.call-start = ((), (), s32[]{:S(2)}) async-start(), calls=%async_computation.4 | async-start | bytes 3899392 | tf_op jit(solution)/shard_map/all_gather | solution.py:26
  7.3 132.5 %all-gather.4.cloned.1.call-start = ((), (), s32[]{:S(2)}) async-start(), calls=%async_computation.2 | async-start | bytes 15597568 | tf_op jit(solution)/shard_map/all_gather | solution.py:20
  8.0 171.9 %all-gather.8.cloned.1.call-start = ((), (), s32[]{:S(2)}) async-start(), calls=%async_computation.6 | async-start | bytes 2228224 | tf_op jit(solution)/shard_map/all_gather | solution.py:27
  8.7 263.3 %all-reduce.2.cloned.1.call-start = ((), (), s32[]{:S(2)}) async-start(), calls=%async_computation.5 | async-start | bytes 131072 | tf_op jit(solution)/shard_map/psum | solution.py:35
  59.9 305.8 %reduce-scatter.2.cloned.1.call-start = ((), (), s32[]{:S(2)}) async-start(), calls=%async_computation.3 | async-start | bytes 8912896 | tf_op jit(solution)/shard_map/reduce_scatter | solution.py:23
  156.3 23.6 %copy-start.1 = (s32[4]{0:T(128)S(1)}, s32[4]{0:T(128)}, u32[]{:S(2)}) copy-start(s32[4]{0:T(128)} %param.10) | copy-start | bytes 52
  156.3 123.4 %copy-start.2 = (s32[4]{0:T(128)S(1)}, s32[4]{0:T(128)}, u32[]{:S(2)}) copy-start(s32[4]{0:T(128)} %param.11) | copy-start | bytes 52
  274.0 14.5 %all-to-all-start = ((bf16[16,32,512]{2,1,0:T(8,128)(2,1)}), bf16[16,32,512]{2,1,0:T(8,128)(2,1)S(1)}, u32[]{:S(2)}, u32[]{:S(2)}) async-start(bf16[16,32,512]{2,1,0:T(8,128)(2,1)} %bitcast.3), calls=%async_computation.1 | async-start | bytes 1048576 | tf_op jit(solution)/shard_map/all_to_all | solution.py:45
Sparse Core Ops, SparseCore 0:
  9.2 44.5 all-gather.5
  55.6 84.1 all-gather.3
  141.6 38.2 all-gather.7
  183.0 89.0 all-reduce.1
  276.0 89.6 reduce-scatter.1
where the time goes:
time: 375 us; the launch traced here: 374 us
  waiting for transfers between devices  325 us (87%)
  matrix products  27.4 us (7%)
  between operations  13.2 us (4%)
  starting transfers between devices  5.89 us (2%)
    psum x1, waiting for transfers between devices, shards(): summed_shrink = lax.psum(shrink.astype(jnp.bfloat16), 'tensor')  89.2 us
    all_gather x1, waiting for transfers between devices, shards(): lax.all_gather(down_weight, 'pool', axis=1, tiled=True)  79.8 us
    reduce_scatter x1, waiting for transfers between devices, shards(): lax.psum_scatter(partial_value.astype(jnp.bfloat16), 'tensor', scatter_di...  77 us
    all_gather x1, waiting for transfers between devices, shards(): shrink_piece = lax.all_gather(adapter_shrink, 'pool', axis=0, tiled=True)  45 us
    all_gather x1, waiting for transfers between devices, shards(): expand_piece = lax.all_gather(adapter_expand, 'pool', axis=0, tiled=True)  23.6 us
    dot_general x1, matrix products, shards(): jnp.dot(hidden, lax.all_gather(down_weight, 'pool', axis=1, tiled=True),...  16.5 us
    all_to_all x1, waiting for transfers between devices, shards(): lax.all_to_all(adapter_delta_columns, 'tensor', split_axis=0, concat_axis...  8.61 us
  transfers between devices with their start and end apart: 6, of which 6 were waited for; matrix products, arithmetic and copies ran while one was open for 7% of the time, Pallas kernels for 0%

commit v1 on v0

--- a/solution.py
+++ b/solution.py
@@ -8,6 +8,22 @@
 
 
 def shards(hidden, down_weight, adapter_shrink, adapter_expand, block_adapter, block_rows):
+
+    def records_check(w_in, inp):
+        a_now, row_out, plain = (lax.axis_size("pool"), lax.axis_index("pool"), w_in.shape[0])
+        field_out, opened = (w_in, None)
+        leaves = tuple(((j0, (j0 + 1) % a_now) for j0 in range(a_now)))
+        for dev_i in range(a_now):
+            s_next = (
+                lax.ppermute(field_out, axis_name="pool", perm=leaves)
+                if dev_i < a_now - 1
+                else None
+            )
+            a_next = inp(field_out, (row_out - dev_i) % a_now * plain)
+            opened = a_next if opened is None else opened + a_next
+            field_out = s_next
+        return opened
+
     input_rows, feat = hidden.shape
     block_count = block_adapter.shape[0]
     column_span = adapter_expand.shape[1]
@@ -24,11 +40,18 @@
         partial_value.astype(jnp.bfloat16), "tensor", scatter_dimension=0, tiled=True
     ).astype(jnp.float32)
     shrink_piece = lax.all_gather(adapter_shrink, "pool", axis=0, tiled=True)
-    expand_piece = lax.all_gather(adapter_expand, "pool", axis=0, tiled=True)
     idents = jnp.arange(shrink_piece.shape[0], dtype=jnp.int32)
     pick = (block_adapter[:, None] == idents[None, :]).astype(jnp.bfloat16)
     first = jnp.einsum("bk,kfr->bfr", pick, shrink_piece, preferred_element_type=jnp.float32)
-    second = jnp.einsum("bk,kcr->bcr", pick, expand_piece, preferred_element_type=jnp.float32)
+    second = records_check(
+        adapter_expand,
+        lambda shard, at: jnp.einsum(
+            "bk,kcr->bcr",
+            lax.dynamic_slice_in_dim(pick, at, shard.shape[0], axis=1),
+            shard,
+            preferred_element_type=jnp.float32,
+        ),
+    )
     shrink = jnp.einsum(
         "bnf,bfr->bnr", blocks, first.astype(jnp.bfloat16), preferred_element_type=jnp.float32
     )

time: 375 us -> 336 us (0.90)
  waiting for transfers between devices: 325 us -> 281 us
    psum x1, waiting for transfers between devices: 89.2 us -> 0.02 us  [shards(): summed_shrink = lax.psum(shrink.astype(jnp.bfloat16), 'tensor')]
    ppermute x0 -> x15, waiting for transfers between devices: none -> 78.2 us  [records_check(): lax.ppermute(field_out, axis_name='pool', perm=leaves)]
    all_gather x1 -> x0, waiting for transfers between devices: 23.6 us -> none  [shards(): expand_piece = lax.all_gather(adapter_expand, 'pool', axis=0, tiled=True)]
    reduce_scatter x1, waiting for transfers between devices: 77 us -> 63.7 us  [shards(): lax.psum_scatter(partial_value.astype(jnp.bfloat16), 'tensor', scatter_di...]
  transfers between devices with their start and end apart: 6 -> 20, of which waited for: 6 -> 19; matrix products, arithmetic and copies ran while one was open for 7% -> 9% of each run, Pallas kernels for 0% -> 0%
where the time goes in v1:
time: 336 us
  waiting for transfers between devices  281 us (84%)
  matrix products  30.2 us (9%)
  between operations  13.4 us (4%)
  starting transfers between devices  7.89 us (2%)
    all_gather x1, waiting for transfers between devices, shards(): lax.all_gather(down_weight, 'pool', axis=1, tiled=True)  79.7 us
    ppermute x15, waiting for transfers between devices, records_check(): lax.ppermute(field_out, axis_name='pool', perm=leaves)  78.2 us
    reduce_scatter x1, waiting for transfers between devices, shards(): lax.psum_scatter(partial_value.astype(jnp.bfloat16), 'tensor', scatter_di...  63.7 us
    all_gather x1, waiting for transfers between devices, shards(): shrink_piece = lax.all_gather(adapter_shrink, 'pool', axis=0, tiled=True)  45.7 us
    dot_general x1, matrix products, shards(): jnp.dot(hidden, lax.all_gather(down_weight, 'pool', axis=1, tiled=True),...  16.5 us
    all_to_all x1, waiting for transfers between devices, shards(): lax.all_to_all(adapter_delta_columns, 'tensor', split_axis=0, concat_axis...  12.2 us
    all_to_all x1, starting transfers between devices, shards(): lax.all_to_all(adapter_delta_columns, 'tensor', split_axis=0, concat_axis...  7.28 us
  transfers between devices with their start and end apart: 20, of which 19 were waited for; matrix products, arithmetic and copies ran while one was open for 9% of the time, Pallas kernels for 0%

profile of v1, /device:TPU:2, one launch (start us, length us, event | category | flops | bytes accessed | tf_op | source)
XLA Modules:
  0.0 335.7 jit_solution(7685385895043934131)
XLA Ops:
  6.5 0.7 all-gather.5.cloned.1.call-update
  7.3 0.7 all-gather.3.cloned.1.call-update
  8.1 45.7 %all-gather.5.cloned.1.call-done = bf16[32,896,64]{1,2,0:T(8,128)(2,1)} async-done(((bf16[2,896,64]{1,2,0:T(8,128)(2,1)}), bf16[32,896,64]{1,2,0:T(8,128)(2,1)}) %all-gather.5.cloned.1.call-update) | async-done | bytes 3670032 | tf_op jit(solution)/shard_map/all_gather | solution.py:42
  53.8 5.0 %fusion.3 = bf16[4,896,64]{1,0,2:T(4,128)(2,1)S(1)} fusion(bf16[32,896,64]{1,2,0:T(8,128)(2,1)} %all-gather.5.cloned.1.call-done, s32[4]{0:T(128)} %param.10), kind=kOutput, calls=%fused_computation.5 | convolution fusion | flops 14909568 | bytes 4128784 | tf_op jit(solution)/shard_map/bk,kfr->bfr/dot_general | solution.py:45
  58.8 1.1 fusion.7
  60.1 79.7 %all-gather.3.cloned.1.call-done = bf16[896,8192]{1,0:T(8,128)(2,1)} async-done(((bf16[896,512]{1,0:T(8,128)(2,1)}), bf16[896,8192]{1,0:T(8,128)(2,1)}) %all-gather.3.cloned.1.call-update) | async-done | bytes 14680080 | tf_op jit(solution)/shard_map/all_gather | solution.py:36
  139.8 16.5 %convolution_convert_fusion = bf16[512,8192]{1,0:T(8,128)(2,1)} fusion(bf16[512,896]{1,0:T(8,128)(2,1)S(1)} %copy-done, bf16[896,8192]{1,0:T(8,128)(2,1)} %all-gather.3.cloned.1.call-done), kind=kOutput, calls=%fused_computation | convolution fusion | flops 7520387072 | bytes 23986176 | tf_op jit(solution)/shard_map/dot_general | solution.py:34
  156.3 0.9 copy-done.1
  157.7 0.4 fusion.12
  158.0 4.9 %collective-permute-done = bf16[2,512,64]{1,0,2:T(2,128)(2,1)S(1)} collective-permute-done((bf16[2,512,64]{1,0,2:T(2,128)(2,1)S(1)}, bf16[2,512,64]{1,0,2:T(2,128)(2,1)S(1)}, u32[]{:S(2)}, u32[]{:S(2)}) %collective-permute-start) | collective-permute-done | bytes 131104 | tf_op jit(solution)/shard_map/ppermute | solution.py:18
  163.3 5.2 %collective-permute-done.1 = bf16[2,512,64]{1,0,2:T(2,128)(2,1)S(1)} collective-permute-done((bf16[2,512,64]{1,0,2:T(2,128)(2,1)S(1)}, bf16[2,512,64]{1,0,2:T(2,128)(2,1)S(1)}, u32[]{:S(2)}, u32[]{:S(2)}) %collective-permute-start.1) | collective-permute-done | bytes 131104 | tf_op jit(solution)/shard_map/ppermute | solution.py:18
  168.9 5.2 %collective-permute-done.2 = bf16[2,512,64]{1,0,2:T(2,128)(2,1)S(1)} collective-permute-done((bf16[2,512,64]{1,0,2:T(2,128)(2,1)S(1)}, bf16[2,512,64]{1,0,2:T(2,128)(2,1)S(1)}, u32[]{:S(2)}, u32[]{:S(2)}) %collective-permute-start.2) | collective-permute-done | bytes 131104 | tf_op jit(solution)/shard_map/ppermute | solution.py:18
  174.5 5.2 %collective-permute-done.3 = bf16[2,512,64]{1,0,2:T(2,128)(2,1)S(1)} collective-permute-done((bf16[2,512,64]{1,0,2:T(2,128)(2,1)S(1)}, bf16[2,512,64]{1,0,2:T(2,128)(2,1)S(1)}, u32[]{:S(2)}, u32[]{:S(2)}) %collective-permute-start.3) | collective-permute-done | bytes 131104 | tf_op jit(solution)/shard_map/ppermute | solution.py:18
  179.7 0.4 convolution_add_fusion.11
  180.1 5.2 %collective-permute-done.4 = bf16[2,512,64]{1,0,2:T(2,128)(2,1)S(1)} collective-permute-done((bf16[2,512,64]{1,0,2:T(2,128)(2,1)S(1)}, bf16[2,512,64]{1,0,2:T(2,128)(2,1)S(1)}, u32[]{:S(2)}, u32[]{:S(2)}) %collective-permute-start.4) | collective-permute-done | bytes 131104 | tf_op jit(solution)/shard_map/ppermute | solution.py:18
  185.7 5.2 %collective-permute-done.5 = bf16[2,512,64]{1,0,2:T(2,128)(2,1)S(1)} collective-permute-done((bf16[2,512,64]{1,0,2:T(2,128)(2,1)S(1)}, bf16[2,512,64]{1,0,2:T(2,128)(2,1)S(1)}, u32[]{:S(2)}, u32[]{:S(2)}) %collective-permute-start.5) | collective-permute-done | bytes 131104 | tf_op jit(solution)/shard_map/ppermute | solution.py:18
  190.9 0.4 convolution_add_fusion.9
  191.3 5.2 %collective-permute-done.6 = bf16[2,512,64]{1,0,2:T(2,128)(2,1)S(1)} collective-permute-done((bf16[2,512,64]{1,0,2:T(2,128)(2,1)S(1)}, bf16[2,512,64]{1,0,2:T(2,128)(2,1)S(1)}, u32[]{:S(2)}, u32[]{:S(2)}) %collective-permute-start.6) | collective-permute-done | bytes 131104 | tf_op jit(solution)/shard_map/ppermute | solution.py:18
  196.9 5.2 %collective-permute-done.7 = bf16[2,512,64]{1,0,2:T(2,128)(2,1)S(1)} collective-permute-done((bf16[2,512,64]{1,0,2:T(2,128)(2,1)S(1)}, bf16[2,512,64]{1,0,2:T(2,128)(2,1)S(1)}, u32[]{:S(2)}, u32[]{:S(2)}) %collective-permute-start.7) | collective-permute-done | bytes 131104 | tf_op jit(solution)/shard_map/ppermute | solution.py:18
  202.5 5.2 %collective-permute-done.8 = bf16[2,512,64]{1,0,2:T(2,128)(2,1)S(1)} collective-permute-done((bf16[2,512,64]{1,0,2:T(2,128)(2,1)S(1)}, bf16[2,512,64]{1,0,2:T(2,128)(2,1)S(1)}, u32[]{:S(2)}, u32[]{:S(2)}) %collective-permute-start.8) | collective-permute-done | bytes 131104 | tf_op jit(solution)/shard_map/ppermute | solution.py:18
  208.1 5.2 %collective-permute-done.9 = bf16[2,512,64]{1,0,2:T(2,128)(2,1)S(1)} collective-permute-done((bf16[2,512,64]{1,0,2:T(2,128)(2,1)S(1)}, bf16[2,512,64]{1,0,2:T(2,128)(2,1)S(1)}, u32[]{:S(2)}, u32[]{:S(2)}) %collective-permute-start.9) | collective-permute-done | bytes 131104 | tf_op jit(solution)/shard_map/ppermute | solution.py:18
  213.7 5.2 %collective-permute-done.10 = bf16[2,512,64]{1,0,2:T(2,128)(2,1)S(1)} collective-permute-done((bf16[2,512,64]{1,0,2:T(2,128)(2,1)S(1)}, bf16[2,512,64]{1,0,2:T(2,128)(2,1)S(1)}, u32[]{:S(2)}, u32[]{:S(2)}) %collective-permute-start.10) | collective-permute-done | bytes 131104 | tf_op jit(solution)/shard_map/ppermute | solution.py:18
  219.3 5.2 %collective-permute-done.11 = bf16[2,512,64]{1,0,2:T(2,128)(2,1)S(1)} collective-permute-done((bf16[2,512,64]{1,0,2:T(2,128)(2,1)S(1)}, bf16[2,512,64]{1,0,2:T(2,128)(2,1)S(1)}, u32[]{:S(2)}, u32[]{:S(2)}) %collective-permute-start.11) | collective-permute-done | bytes 131104 | tf_op jit(solution)/shard_map/ppermute | solution.py:18
  224.9 5.2 %collective-permute-done.12 = bf16[2,512,64]{1,0,2:T(2,128)(2,1)S(1)} collective-permute-done((bf16[2,512,64]{1,0,2:T(2,128)(2,1)S(1)}, bf16[2,512,64]{1,0,2:T(2,128)(2,1)S(1)}, u32[]{:S(2)}, u32[]{:S(2)}) %collective-permute-start.12) | collective-permute-done | bytes 131104 | tf_op jit(solution)/shard_map/ppermute | solution.py:18
  230.2 0.4 convolution_add_fusion.2
  230.5 5.2 %collective-permute-done.13 = bf16[2,512,64]{1,0,2:T(2,128)(2,1)S(1)} collective-permute-done((bf16[2,512,64]{1,0,2:T(2,128)(2,1)S(1)}, bf16[2,512,64]{1,0,2:T(2,128)(2,1)S(1)}, u32[]{:S(2)}, u32[]{:S(2)}) %collective-permute-start.13) | collective-permute-done | bytes 131104 | tf_op jit(solution)/shard_map/ppermute | solution.py:18
  236.1 5.2 %collective-permute-done.14 = bf16[2,512,64]{1,0,2:T(2,128)(2,1)S(1)} collective-permute-done((bf16[2,512,64]{1,0,2:T(2,128)(2,1)S(1)}, bf16[2,512,64]{1,0,2:T(2,128)(2,1)S(1)}, u32[]{:S(2)}, u32[]{:S(2)}) %collective-permute-start.14) | collective-permute-done | bytes 131104 | tf_op jit(solution)/shard_map/ppermute | solution.py:18
  241.8 2.0 fusion.2
  243.7 7.3 %all-to-all-start = ((bf16[16,32,512]{2,1,0:T(8,128)(2,1)}), bf16[16,32,512]{2,1,0:T(8,128)(2,1)S(1)}, u32[]{:S(2)}, u32[]{:S(2)}) async-start(bf16[16,32,512]{2,1,0:T(8,128)(2,1)} %bitcast.19), calls=%async_computation.1 | async-start | bytes 1048576 | tf_op jit(solution)/shard_map/all_to_all | solution.py:68
  251.1 12.2 %all-to-all-done = bf16[16,32,512]{2,1,0:T(8,128)(2,1)S(1)} async-done(((bf16[16,32,512]{2,1,0:T(8,128)(2,1)}), bf16[16,32,512]{2,1,0:T(8,128)(2,1)S(1)}, u32[]{:S(2)}, u32[]{:S(2)}) %all-to-all-start) | async-done | bytes 524320 | tf_op jit(solution)/shard_map/all_to_all | solution.py:68
  263.5 63.7 %reduce-scatter.2.cloned.1.call-done = bf16[32,8192]{1,0:T(8,128)(2,1)} async-done(((bf16[512,8192]{1,0:T(8,128)(2,1)}), bf16[32,8192]{1,0:T(8,128)(2,1)}) %reduce-scatter.2.cloned.1.call-update) | async-done | bytes 524304 | tf_op jit(solution)/shard_map/reduce_scatter | solution.py:39
  327.2 2.0 multiply_convert_fusion
  (48 shorter events, 5.4 us)
Async XLA Ops:
  6.5 52.2 %copy-start = (bf16[512,896]{1,0:T(8,128)(2,1)S(1)}, bf16[512,896]{1,0:T(8,128)(2,1)}, u32[]{:S(2)}) copy-start(bf16[512,896]{1,0:T(8,128)(2,1)} %param.6) | copy-start | bytes 2752516
  6.5 47.2 %all-gather.5.cloned.1.call-start = ((), (), s32[]{:S(2)}) async-start(), calls=%async_computation.4 | async-start | bytes 3899392 | tf_op jit(solution)/shard_map/all_gather | solution.py:42
  7.3 132.5 %all-gather.3.cloned.1.call-start = ((), (), s32[]{:S(2)}) async-start(), calls=%async_computation.2 | async-start | bytes 15597568 | tf_op jit(solution)/shard_map/all_gather | solution.py:36
  8.0 233.7 %all-reduce.2.cloned.1.call-start = ((), (), s32[]{:S(2)}) async-start(), calls=%async_computation.5 | async-start | bytes 131072 | tf_op jit(solution)/shard_map/psum | solution.py:58
  59.9 267.3 %reduce-scatter.2.cloned.1.call-start = ((), (), s32[]{:S(2)}) async-start(), calls=%async_computation.3 | async-start | bytes 8912896 | tf_op jit(solution)/shard_map/reduce_scatter | solution.py:39
  156.2 0.9 copy-start.1
  156.2 1.4 copy-start.2
  157.3 5.6 %collective-permute-start = (bf16[2,512,64]{1,0,2:T(2,128)(2,1)S(1)}, bf16[2,512,64]{1,0,2:T(2,128)(2,1)S(1)}, u32[]{:S(2)}, u32[]{:S(2)}) collective-permute-start(bf16[2,512,64]{1,0,2:T(2,128)(2,1)S(1)} %copy.12), channel_id=1, source_target_pairs={{0,16},{16,32},{32,48},{48,64},{64,80},{80,96},{96,112},{112,128},... | collective-permute-start | bytes 393224 | tf_op jit(solution)/shard_map/ppermute | solution.py:18
  162.9 5.6 %collective-permute-start.1 = (bf16[2,512,64]{1,0,2:T(2,128)(2,1)S(1)}, bf16[2,512,64]{1,0,2:T(2,128)(2,1)S(1)}, u32[]{:S(2)}, u32[]{:S(2)}) collective-permute-start(bf16[2,512,64]{1,0,2:T(2,128)(2,1)S(1)} %collective-permute-done), channel_id=1, source_target_pairs={{0,16},{16,32},{32,48},{48,64},{64,80},{80,96},{96,112},{112,128},... | collective-permute-start | bytes 393224 | tf_op jit(solution)/shard_map/ppermute | solution.py:18
  168.5 5.6 %collective-permute-start.2 = (bf16[2,512,64]{1,0,2:T(2,128)(2,1)S(1)}, bf16[2,512,64]{1,0,2:T(2,128)(2,1)S(1)}, u32[]{:S(2)}, u32[]{:S(2)}) collective-permute-start(bf16[2,512,64]{1,0,2:T(2,128)(2,1)S(1)} %collective-permute-done.1), channel_id=1, source_target_pairs={{0,16},{16,32},{32,48},{48,64},{64,80},{80,96},{96,112},{112,128},... | collective-permute-start | bytes 393224 | tf_op jit(solution)/shard_map/ppermute | solution.py:18
  168.9 82.2 %copy-start.3 = (s32[4]{0:T(128)S(1)}, s32[4]{0:T(128)}, u32[]{:S(2)}) copy-start(s32[4]{0:T(128)} %param.11) | copy-start | bytes 52
  174.1 5.6 %collective-permute-start.3 = (bf16[2,512,64]{1,0,2:T(2,128)(2,1)S(1)}, bf16[2,512,64]{1,0,2:T(2,128)(2,1)S(1)}, u32[]{:S(2)}, u32[]{:S(2)}) collective-permute-start(bf16[2,512,64]{1,0,2:T(2,128)(2,1)S(1)} %collective-permute-done.2), channel_id=1, source_target_pairs={{0,16},{16,32},{32,48},{48,64},{64,80},{80,96},{96,112},{112,128},... | collective-permute-start | bytes 393224 | tf_op jit(solution)/shard_map/ppermute | solution.py:18
  179.7 5.6 %collective-permute-start.4 = (bf16[2,512,64]{1,0,2:T(2,128)(2,1)S(1)}, bf16[2,512,64]{1,0,2:T(2,128)(2,1)S(1)}, u32[]{:S(2)}, u32[]{:S(2)}) collective-permute-start(bf16[2,512,64]{1,0,2:T(2,128)(2,1)S(1)} %collective-permute-done.3), channel_id=1, source_target_pairs={{0,16},{16,32},{32,48},{48,64},{64,80},{80,96},{96,112},{112,128},... | collective-permute-start | bytes 393224 | tf_op jit(solution)/shard_map/ppermute | solution.py:18
  185.3 5.6 %collective-permute-start.5 = (bf16[2,512,64]{1,0,2:T(2,128)(2,1)S(1)}, bf16[2,512,64]{1,0,2:T(2,128)(2,1)S(1)}, u32[]{:S(2)}, u32[]{:S(2)}) collective-permute-start(bf16[2,512,64]{1,0,2:T(2,128)(2,1)S(1)} %collective-permute-done.4), channel_id=1, source_target_pairs={{0,16},{16,32},{32,48},{48,64},{64,80},{80,96},{96,112},{112,128},... | collective-permute-start | bytes 393224 | tf_op jit(solution)/shard_map/ppermute | solution.py:18
  190.9 5.6 %collective-permute-start.6 = (bf16[2,512,64]{1,0,2:T(2,128)(2,1)S(1)}, bf16[2,512,64]{1,0,2:T(2,128)(2,1)S(1)}, u32[]{:S(2)}, u32[]{:S(2)}) collective-permute-start(bf16[2,512,64]{1,0,2:T(2,128)(2,1)S(1)} %collective-permute-done.5), channel_id=1, source_target_pairs={{0,16},{16,32},{32,48},{48,64},{64,80},{80,96},{96,112},{112,128},... | collective-permute-start | bytes 393224 | tf_op jit(solution)/shard_map/ppermute | solution.py:18
  196.5 5.6 %collective-permute-start.7 = (bf16[2,512,64]{1,0,2:T(2,128)(2,1)S(1)}, bf16[2,512,64]{1,0,2:T(2,128)(2,1)S(1)}, u32[]{:S(2)}, u32[]{:S(2)}) collective-permute-start(bf16[2,512,64]{1,0,2:T(2,128)(2,1)S(1)} %collective-permute-done.6), channel_id=1, source_target_pairs={{0,16},{16,32},{32,48},{48,64},{64,80},{80,96},{96,112},{112,128},... | collective-permute-start | bytes 393224 | tf_op jit(solution)/shard_map/ppermute | solution.py:18
  202.1 5.6 %collective-permute-start.8 = (bf16[2,512,64]{1,0,2:T(2,128)(2,1)S(1)}, bf16[2,512,64]{1,0,2:T(2,128)(2,1)S(1)}, u32[]{:S(2)}, u32[]{:S(2)}) collective-permute-start(bf16[2,512,64]{1,0,2:T(2,128)(2,1)S(1)} %collective-permute-done.7), channel_id=1, source_target_pairs={{0,16},{16,32},{32,48},{48,64},{64,80},{80,96},{96,112},{112,128},... | collective-permute-start | bytes 393224 | tf_op jit(solution)/shard_map/ppermute | solution.py:18
  207.7 5.6 %collective-permute-start.9 = (bf16[2,512,64]{1,0,2:T(2,128)(2,1)S(1)}, bf16[2,512,64]{1,0,2:T(2,128)(2,1)S(1)}, u32[]{:S(2)}, u32[]{:S(2)}) collective-permute-start(bf16[2,512,64]{1,0,2:T(2,128)(2,1)S(1)} %collective-permute-done.8), channel_id=1, source_target_pairs={{0,16},{16,32},{32,48},{48,64},{64,80},{80,96},{96,112},{112,128},... | collective-permute-start | bytes 393224 | tf_op jit(solution)/shard_map/ppermute | solution.py:18
  213.3 5.6 %collective-permute-start.10 = (bf16[2,512,64]{1,0,2:T(2,128)(2,1)S(1)}, bf16[2,512,64]{1,0,2:T(2,128)(2,1)S(1)}, u32[]{:S(2)}, u32[]{:S(2)}) collective-permute-start(bf16[2,512,64]{1,0,2:T(2,128)(2,1)S(1)} %collective-permute-done.9), channel_id=1, source_target_pairs={{0,16},{16,32},{32,48},{48,64},{64,80},{80,96},{96,112},{112,128},... | collective-permute-start | bytes 393224 | tf_op jit(solution)/shard_map/ppermute | solution.py:18
  218.9 5.6 %collective-permute-start.11 = (bf16[2,512,64]{1,0,2:T(2,128)(2,1)S(1)}, bf16[2,512,64]{1,0,2:T(2,128)(2,1)S(1)}, u32[]{:S(2)}, u32[]{:S(2)}) collective-permute-start(bf16[2,512,64]{1,0,2:T(2,128)(2,1)S(1)} %collective-permute-done.10), channel_id=1, source_target_pairs={{0,16},{16,32},{32,48},{48,64},{64,80},{80,96},{96,112},{112,128},... | collective-permute-start | bytes 393224 | tf_op jit(solution)/shard_map/ppermute | solution.py:18
  224.5 5.6 %collective-permute-start.12 = (bf16[2,512,64]{1,0,2:T(2,128)(2,1)S(1)}, bf16[2,512,64]{1,0,2:T(2,128)(2,1)S(1)}, u32[]{:S(2)}, u32[]{:S(2)}) collective-permute-start(bf16[2,512,64]{1,0,2:T(2,128)(2,1)S(1)} %collective-permute-done.11), channel_id=1, source_target_pairs={{0,16},{16,32},{32,48},{48,64},{64,80},{80,96},{96,112},{112,128},... | collective-permute-start | bytes 393224 | tf_op jit(solution)/shard_map/ppermute | solution.py:18
  230.2 5.6 %collective-permute-start.13 = (bf16[2,512,64]{1,0,2:T(2,128)(2,1)S(1)}, bf16[2,512,64]{1,0,2:T(2,128)(2,1)S(1)}, u32[]{:S(2)}, u32[]{:S(2)}) collective-permute-start(bf16[2,512,64]{1,0,2:T(2,128)(2,1)S(1)} %collective-permute-done.12), channel_id=1, source_target_pairs={{0,16},{16,32},{32,48},{48,64},{64,80},{80,96},{96,112},{112,128},... | collective-permute-start | bytes 393224 | tf_op jit(solution)/shard_map/ppermute | solution.py:18
  235.8 5.6 %collective-permute-start.14 = (bf16[2,512,64]{1,0,2:T(2,128)(2,1)S(1)}, bf16[2,512,64]{1,0,2:T(2,128)(2,1)S(1)}, u32[]{:S(2)}, u32[]{:S(2)}) collective-permute-start(bf16[2,512,64]{1,0,2:T(2,128)(2,1)S(1)} %collective-permute-done.13), channel_id=1, source_target_pairs={{0,16},{16,32},{32,48},{48,64},{64,80},{80,96},{96,112},{112,128},... | collective-permute-start | bytes 393224 | tf_op jit(solution)/shard_map/ppermute | solution.py:18
  243.7 19.6 %all-to-all-start = ((bf16[16,32,512]{2,1,0:T(8,128)(2,1)}), bf16[16,32,512]{2,1,0:T(8,128)(2,1)S(1)}, u32[]{:S(2)}, u32[]{:S(2)}) async-start(bf16[16,32,512]{2,1,0:T(8,128)(2,1)} %bitcast.19), calls=%async_computation.1 | async-start | bytes 1048576 | tf_op jit(solution)/shard_map/all_to_all | solution.py:68
Sparse Core Ops, SparseCore 0:
  9.2 44.5 all-gather.4
  55.6 84.1 all-gather.2
  143.0 89.2 all-reduce.1
  236.3 90.8 reduce-scatter.1
